TPU v7x, 256 devices: a whole 4x4x8 slice. The times are simulated.
256 devices in a mesh: row: 32 (over y, x, core), col: 8 (over z).
Axes of the slice: x: 4, y: 4, z: 8, core: 2. Of those that a mesh axis runs over, the one named last changes fastest.
Arguments:
- diag_block: float32 [512, 512], P(('row', 'col')), may hold values from 0 to 2, as said below
- panel_block: float32 [8192, 512], P('row', 'col'), may hold values from 0 to 1, as said below
- trailing: float32 [8192, 8192], P('row', 'col'), may hold values from 0 to 2, as said below
Outputs:
- factor_diag: float32 [512, 512], P(('row', 'col'))
- factor_panel: float32 [8192, 512], P('row', 'col')
- schur: float32 [8192, 8192], P('row', 'col')
Inputs may be any that keep to these rules, and one draw needn't show every extreme that they name: diag_block is symmetric positive definite: a covariance matrix plus the identity. panel_block holds the covariances between slab points and panel points of the same covariance. trailing is symmetric, and together with diag_block and panel_block forms one positive definite covariance matrix plus the identity.
All inputs are finite; a program needn't handle non-finite values.
Results may differ from a plain program's by a relative error of at most 0.00028.
Values sent between devices are 32-bit elements; how exact they have to be, the bound alone decides.
A program may use at most 64 MiB of HBM per device.

v0:
```python
import jax
import jax.numpy as jnp
from jax import lax
from jax.sharding import PartitionSpec as P


def forward(factor, rows_in):
    return jax.scipy.linalg.solve_triangular(factor, rows_in.T, lower=True).T


def per_device(diag_block, panel_block, trailing):
    col_count = lax.axis_size("col")
    row_index = lax.axis_index("row")
    col_index = lax.axis_index("col")
    gathered = lax.all_gather(diag_block, ("row", "col"), axis=0, tiled=True)
    factor = jnp.linalg.cholesky(gathered)
    diag_rows_here = diag_block.shape[0]
    diag_part = lax.dynamic_slice_in_dim(
        factor, (row_index * col_count + col_index) * diag_rows_here, diag_rows_here, 0
    )
    full_rows = lax.all_gather(panel_block, "col", axis=1, tiled=True)
    solved = forward(factor, full_rows)
    panel_width = panel_block.shape[1]
    panel_part = lax.dynamic_slice_in_dim(solved, col_index * panel_width, panel_width, 1)
    col_span = trailing.shape[1]
    all_rows = lax.all_gather(solved, "row", axis=0, tiled=True)
    column_factor = lax.dynamic_slice_in_dim(all_rows, col_index * col_span, col_span, 0)
    update = lax.dot_general(
        solved,
        column_factor,
        (((1,), (1,)), ((), ())),
        precision=lax.Precision.HIGHEST,
        preferred_element_type=jnp.float32,
    )
    return (diag_part, panel_part, trailing - update)


def solution(mesh):
    return jax.shard_map(
        per_device,
        mesh=mesh,
        in_specs=(P(("row", "col"), None), P("row", "col"), P("row", "col")),
        out_specs=(P(("row", "col"), None), P("row", "col"), P("row", "col")),
        check_vma=False,
    )
```

profile of v0, /device:TPU:1, one launch (start us, length us, event | category | flops | bytes accessed | tf_op | source)
XLA Modules:
  0.0 354.9 jit_solution(7039044889114310053)
XLA Ops:
  7.2 0.7 all-gather.6.cloned.1.call-update
  8.0 26.5 %all_gather.10 = f32[256,512]{0,1:T(8,128)} all-gather(f32[256,64]{0,1:T(8,128)} %param.4), channel_id=1, replica_groups=mesh['row'=32,'col'=8] {'col'}, dimensions={1}, use_global_device_ids=true | all-gather | bytes 589824 | tf_op jit(solution)/shard_map/all_gather | solution.py:21
  34.4 84.4 %all-gather.6.cloned.1.call-done = f32[256,2,512]{2,1,0:T(2,128)} async-done(((f32[1,2,512]{2,1,0:T(2,128)}), f32[256,2,512]{2,1,0:T(2,128)}) %all-gather.6.cloned.1.call-update) | async-done | bytes 1048592 | tf_op jit(solution)/shard_map/all_gather | solution.py:15
  118.8 1.9 reshape.65
  120.8 0.3 copy.9
  121.1 0.2 fusion.5
  121.4 11.7 %cholesky.104 = f32[128,128]{1,0:T(8,128)S(1)} custom-call(f32[128,128]{1,0:T(8,128)S(1)} %cholesky.266), custom_call_target="Cholesky" | custom-call | tf_op jit(solution)/shard_map/jit(cholesky)/cholesky | solution.py:16
  133.1 0.1 cholesky.224
  133.2 9.8 %custom-call.31 = f32[1,128,128]{1,2,0:T(8,128)S(1)} custom-call(f32[1,128,128]{2,1,0:T(8,128)S(1)} %get-tuple-element.34), custom_call_target="InvertDiagBlocksLowerTriangular" | custom-call | tf_op jit(solution)/shard_map/jit(cholesky)/cholesky | solution.py:16
  143.0 0.3 constant_dynamic-update-slice_fusion.1
  143.4 0.3 convolution_subtract_fusion
  143.7 11.7 %cholesky.217 = f32[128,128]{1,0:T(8,128)S(1)} custom-call(f32[128,128]{1,0:T(8,128)S(1)} %cholesky.270), custom_call_target="Cholesky" | custom-call | tf_op jit(solution)/shard_map/jit(cholesky)/cholesky | solution.py:16
  155.5 9.9 %custom-call.32 = f32[1,128,128]{1,2,0:T(8,128)S(1)} custom-call(f32[1,128,128]{2,1,0:T(8,128)S(1)} %get-tuple-element.31), custom_call_target="InvertDiagBlocksLowerTriangular" | custom-call | tf_op jit(solution)/shard_map/jit(cholesky)/cholesky | solution.py:16
  165.4 0.3 convolution_dynamic-update-slice_fusion
  165.7 0.4 convolution_subtract_fusion.3
  166.1 11.7 %cholesky.238 = f32[128,128]{1,0:T(8,128)S(1)} custom-call(f32[128,128]{1,0:T(8,128)S(1)} %cholesky.275), custom_call_target="Cholesky" | custom-call | tf_op jit(solution)/shard_map/jit(cholesky)/cholesky | solution.py:16
  177.8 9.8 %custom-call.33 = f32[1,128,128]{1,2,0:T(8,128)S(1)} custom-call(f32[1,128,128]{2,1,0:T(8,128)S(1)} %get-tuple-element.28), custom_call_target="InvertDiagBlocksLowerTriangular" | custom-call | tf_op jit(solution)/shard_map/jit(cholesky)/cholesky | solution.py:16
  187.6 0.2 convolution_dynamic-update-slice_fusion.1
  187.8 0.4 convolution_subtract_fusion.5
  188.2 11.9 %cholesky.255 = f32[128,128]{1,0:T(8,128)S(1)} custom-call(f32[128,128]{1,0:T(8,128)S(1)} %convolution_subtract_fusion.5), custom_call_target="Cholesky" | custom-call | tf_op jit(solution)/shard_map/jit(cholesky)/cholesky | solution.py:16
  200.2 0.6 compare_reduce_fusion.1
  200.8 0.7 compare_reduce_fusion
  201.5 0.6 compare_reduce_fusion.2
  204.8 0.3 fusion.6
  205.1 8.0 %while.1 = (s32[]{:T(128)}, f32[512,512]{1,0:T(8,128)S(1)}, s32[4,2]{0,1:T(2,128)S(1)}, f32[4,128,128]{2,1,0:T(8,128)S(1)}, s32[]{:T(128)}) while((s32[]{:T(128)}, f32[512,512]{1,0:T(8,128)S(1)}, s32[4,2]{0,1:T(2,128)S(1)}, f32[4,128,128]{2,1,0:T(8,128)S(1)}, s32[]{:T(128)}) %tuple.33), condition=%wide.while_cond, body=%wide.while_body.sunk | while | flops 2 | bytes 131189 | solution.py:8
  205.1 0.1 constant_dynamic-slice_fusion.3
  205.2 0.5 fusion.45
  205.7 1.4 bitcast_dynamic-update-slice_fusion.2
  207.2 0.5 fusion.45
  207.7 1.4 bitcast_dynamic-update-slice_fusion.2
  209.2 0.5 fusion.45
  209.7 1.4 bitcast_dynamic-update-slice_fusion.2
  211.1 0.1 constant_dynamic-slice_fusion.3
  211.2 0.5 fusion.45
  211.7 1.4 bitcast_dynamic-update-slice_fusion.2
  213.1 39.3 %custom-call.34 = f32[4,128,128]{1,2,0:T(8,128)S(1)} custom-call(f32[4,128,128]{2,1,0:T(8,128)S(1)} %get-tuple-element.10), custom_call_target="InvertDiagBlocksLowerTriangular" | custom-call | tf_op jit(solution)/shard_map/jit(_solve_triangular)/triangular_solve | solution.py:8
  252.4 1.2 fusion.21
  253.7 1.2 convolution_subtract_fusion.4
  254.8 0.3 fusion.28
  255.1 1.2 convolution_subtract_fusion.2
  256.3 0.3 fusion.26
  256.7 1.3 convolution_subtract_fusion.1
  258.0 0.3 fusion.25
  258.3 0.9 fusion.37
  259.2 0.6 constant_dynamic-slice_fusion.1
  259.8 0.6 dynamic-slice_bitcast_fusion
  260.4 82.9 %all-gather.4.cloned.1.call-done = f32[8192,512]{0,1:T(8,128)} async-done(((f32[256,512]{0,1:T(8,128)}), f32[8192,512]{0,1:T(8,128)}) %all-gather.4.cloned.1.call-update) | async-done | bytes 16777232 | tf_op jit(solution)/shard_map/all_gather | solution.py:26
  343.3 4.7 %fusion.2 = f32[256,1024]{1,0:T(8,128)} fusion(f32[256,1024]{1,0:T(8,128)} %param.5, f32[8192,512]{0,1:T(8,128)} %all-gather.4.cloned.1.call-done, s32[]{:T(128)S(6)} %select_n.16, f32[128,256]{1,0:T(8,128)S(1)} %fusion.25, f32[128,256]{1,0:T(8,128)S(1)} %fusion.26, f32[128,256]{1,0:T(8,128)S(1)} %fusion.28, f32[128,256]{1,0:T(8,128)S(1)} %fusion.21), kind=kOutput, calls=%fused_computation.4 | convolution fusion | flops 1611268096 | bytes 4718596 | tf_op jit(solution)/shard_map/dot_general | solution.py:28
  (15 shorter events, 0.4 us)
Async XLA Ops:
  7.2 111.7 %all-gather.6.cloned.1.call-start = ((), (), s32[]{:S(2)}) async-start(), calls=%async_computation.1 | async-start | bytes 1052672 | tf_op jit(solution)/shard_map/all_gather | solution.py:15
  7.9 335.4 %all-gather.4.cloned.1.call-start = ((), (), s32[]{:S(2)}) async-start(), calls=%async_computation | async-start | bytes 17301504 | tf_op jit(solution)/shard_map/all_gather | solution.py:26
Sparse Core Ops, SparseCore 0:
  11.7 107.0 all-gather.5
  259.3 84.0 all-gather.3
where the time goes:
time: 355 us
  waiting for transfers between devices  168 us (47%)
  other arithmetic  119 us (34%)
  blocking collectives  26.5 us (7%)
  between operations  16.9 us (5%)
  matrix products  12.3 us (3%)
  local copies, waits for them, and re-layouts  11.6 us (3%)
    all_gather x1, waiting for transfers between devices, per_device(): gathered = lax.all_gather(diag_block, ('row', 'col'), axis=0, tiled=True)  84.4 us
    all_gather x1, waiting for transfers between devices, per_device(): all_rows = lax.all_gather(solved, 'row', axis=0, tiled=True)  82.9 us
    another operation x14, other arithmetic, per_device(): factor = jnp.linalg.cholesky(gathered)  78.7 us
    another operation x3, other arithmetic, forward(): return jax.scipy.linalg.solve_triangular(factor, rows_in.T, lower=True).T  39.6 us
    all_gather x1, blocking collectives, per_device(): full_rows = lax.all_gather(panel_block, 'col', axis=1, tiled=True)  26.5 us
    another operation x12, local copies, waits for them, and re-layouts  7.92 us
  transfers between devices with their start and end apart: 2, of which 2 were waited for; matrix products, arithmetic and copies ran while one was open for 0% of the time, Pallas kernels for 0%

commit v1 on v0

v1 whole, which is shorter than its diff:
```python
import functools

import jax
import jax.numpy as jnp
from jax import lax
from jax.experimental import pallas as pl
from jax.experimental.pallas import tpu as pltpu
from jax.sharding import PartitionSpec as P

NB = 512
F32 = jnp.float32
BF16 = jnp.bfloat16
MESH = pl.DeviceIdType.MESH
CHIPS = 16
COLS = 8


def gather_kernel(a_ref, b_ref, g_ref, br_ref, bc_ref, m_ref,
                  as_sem, ar_sem, rs_sem, rr_sem, ms_sem, mr_sem, ps_sem, pr_sem, loc_sem):
    row = lax.axis_index("row")
    z = lax.axis_index("col")
    chip = row // 2
    core = row % 2

    def at_z(k):
        return {"row": row, "col": (z + k) % COLS}

    def at_chip(k):
        return {"row": ((chip + k) % CHIPS) * 2 + core, "col": z}

    partner = {"row": row + 1 - 2 * core, "col": z}

    def copy(src, dst, ssem, rsem, device):
        return pltpu.make_async_remote_copy(
            src_ref=src, dst_ref=dst, send_sem=ssem, recv_sem=rsem,
            device_id=device, device_id_type=MESH)

    barrier = pltpu.get_barrier_semaphore()
    for k in range(1, COLS):
        pl.semaphore_signal(barrier, inc=1, device_id=at_z(k), device_id_type=MESH)
    for k in range(1, CHIPS):
        pl.semaphore_signal(barrier, inc=1, device_id=at_chip(k), device_id_type=MESH)
    pl.semaphore_signal(barrier, inc=1, device_id=partner, device_id_type=MESH)
    own_a = pltpu.make_async_copy(a_ref, g_ref.at[chip, core, z], loc_sem.at[0])
    own_b = pltpu.make_async_copy(b_ref, br_ref.at[z], loc_sem.at[1])
    own_a.start()
    own_b.start()
    pl.semaphore_wait(barrier, COLS + CHIPS - 1)

    a_z = [copy(a_ref, g_ref.at[chip, core, z], as_sem.at[k - 1], ar_sem.at[k - 1], at_z(k))
           for k in range(1, COLS)]
    for c in a_z:
        c.start()

    move1 = copy(b_ref, m_ref, ms_sem.at[0], mr_sem.at[0], at_chip(2 * z))
    move1_own = pltpu.make_async_copy(b_ref, m_ref, loc_sem.at[2])

    @pl.when(z != 0)
    def _():
        move1.start()

    @pl.when(z == 0)
    def _():
        move1_own.start()

    own_a.wait()
    for c in a_z:
        c.wait()
    mine = g_ref.at[chip, core]
    a_p = [copy(mine, mine, as_sem.at[6 + k], ar_sem.at[6 + k], at_chip(k))
           for k in range(1, CHIPS)]
    for c in a_p:
        c.start()

    @pl.when(z != 0)
    def _():
        move1.wait()

    @pl.when(z == 0)
    def _():
        move1_own.wait()

    src = (chip + CHIPS - 2 * z) % CHIPS
    plane = src // 2
    slot = bc_ref.at[src % 2, core, z]
    move2 = copy(m_ref, slot, ms_sem.at[1], mr_sem.at[1], {"row": row, "col": plane})
    move2_own = pltpu.make_async_copy(m_ref, slot, loc_sem.at[3])

    @pl.when(plane != z)
    def _():
        move2.start()

    @pl.when(plane == z)
    def _():
        move2_own.start()

    b_z = [copy(b_ref, br_ref.at[z], rs_sem.at[k - 1], rr_sem.at[k - 1], at_z(k))
           for k in range(1, COLS)]
    for c in b_z:
        c.start()

    for c in a_p:
        c.wait()
    half = g_ref.at[:, core]
    a_c = copy(half, half, as_sem.at[22], ar_sem.at[22], partner)
    a_c.start()

    @pl.when(plane != z)
    def _():
        move2.wait()

    @pl.when(plane == z)
    def _():
        move2_own.wait()

    held = bc_ref.at[chip % 2, core, (chip // 2 + COLS - z) % COLS]
    b_p = [copy(held, held, ps_sem.at[k - 1], pr_sem.at[k - 1], at_chip(k))
           for k in range(1, CHIPS)]
    for c in b_p:
        c.start()
    a_c.wait()
    for c in b_p:
        c.wait()
    bhalf = bc_ref.at[:, core]
    b_c = copy(bhalf, bhalf, ps_sem.at[15], pr_sem.at[15], partner)
    b_c.start()
    own_b.wait()
    for c in b_z:
        c.wait()
    b_c.wait()


def gather(a_tile, b_t):
    vmem = pl.BlockSpec(memory_space=pltpu.VMEM)
    dma = pltpu.SemaphoreType.DMA
    return pl.pallas_call(
        gather_kernel,
        out_shape=(
            jax.ShapeDtypeStruct((CHIPS, 2, COLS, 8, 128), F32),
            jax.ShapeDtypeStruct((COLS, 64, 256), F32),
            jax.ShapeDtypeStruct((2, 2, COLS, 64, 256), F32),
        ),
        in_specs=[vmem] * 2,
        out_specs=(vmem,) * 3,
        scratch_shapes=[
            pltpu.VMEM((64, 256), F32),
            dma((23,)), dma((23,)), dma((7,)), dma((7,)), dma((2,)), dma((2,)),
            dma((16,)), dma((16,)), dma((4,)),
        ],
        compiler_params=pltpu.CompilerParams(collective_id=0, has_side_effects=True),
        name="gather",
    )(a_tile, b_t)


def split(x):
    high = x.astype(BF16)
    return high, (x - high.astype(F32)).astype(BF16)


def mm(a, b, dims):
    return lax.dot_general(a, b, (dims, ((), ())), preferred_element_type=F32)


NN = ((1,), (0,))
NT = ((1,), (1,))


def dot3s(a, b, dims=NN):
    return mm(a[0], b[0], dims) + (mm(a[0], b[1], dims) + mm(a[1], b[0], dims))


def dot3(a, b, dims=NN):
    return dot3s(split(a), split(b), dims)


def scales(top, tol):
    e = (top - 1.0) / (top + 1.0)
    out = []
    while e > tol:
        m = 2.0 / (2.0 - e * e)
        out.append(m)
        e = e * e * m / 2.0
    return 2.0 / (1.0 + top), out


def eye(n):
    return (lax.broadcasted_iota(jnp.int32, (n, n), 0)
            == lax.broadcasted_iota(jnp.int32, (n, n), 1)).astype(F32)


TOL = 3e-3


def inverse(mats, top, one):
    start, steps = scales(top, TOL)
    n = one.shape[0]
    xs = [None] * len(mats)
    rs = [start * m for m in mats]
    for k, m in enumerate(steps):
        last = k == len(steps) - 1
        ns = [(2.0 * m) * one - m * r for r in rs]
        if k == 0:
            xs = [start * nn for nn in ns]
            if not last:
                rs = [dot3(r, nn) for r, nn in zip(rs, ns)]
        elif last:
            xs = [dot3(x, nn) for x, nn in zip(xs, ns)]
        else:
            both = [dot3(jnp.concatenate([x, r], 0), nn) for x, r, nn in zip(xs, rs, ns)]
            xs = [t[:n] for t in both]
            rs = [t[n:] for t in both]
    return xs


def tri_low(n):
    i = lax.broadcasted_iota(jnp.int32, (n, n), 0)
    j = lax.broadcasted_iota(jnp.int32, (n, n), 1)
    return i, j


def factor_kernel(g_ref, br_ref, bc_ref, t_ref, fd_ref, fp_ref, s_ref, a4_ref, a_ref, w_ref, l_ref):
    row = lax.axis_index("row")
    z = lax.axis_index("col")
    for s in range(2):
        for l in range(4):
            a4_ref[l, pl.ds(s, 256, stride=2), :] = (
                g_ref[pl.ds(2 * l + s, 256, stride=8), :])
    for l in range(4):
        a_ref[:, l * 128:(l + 1) * 128] = a4_ref[l]
    one256 = eye(256)
    one128 = eye(128)
    a11 = a_ref[0:256, 0:256]
    a21 = a_ref[256:512, 0:256]
    x = inverse([a11], 257.0, one256)[0]
    g1 = dot3(a21, x)
    blocks = [a11, a_ref[256:512, 256:512] - dot3(g1, a21, NT)]
    xs = inverse([m[:128, :128] for m in blocks], 129.0, one128)
    tiles = []
    g2 = []
    for m, x in zip(blocks, xs):
        low = m[128:, :128]
        g = dot3(low, x)
        g2.append(g)
        tiles += [m[:128, :128], m[128:, 128:] - dot3(g, low, NT)]
    g1p = jnp.concatenate([g1[:128], g1[128:] - dot3(g2[1], g1[:128])], 0)
    i, j = tri_low(128)
    ts = None
    b = 64
    while b >= 1:
        bi, bj = i // b, j // b
        same = bi == bj
        even = bi % 2 == 0
        m21 = jnp.logical_and(bi == bj + 1, bj % 2 == 0)
        lows = [jnp.where(m21, m, 0.0) for m in tiles]
        odd_one = jnp.where(even, 0.0, one128)
        keep = jnp.logical_and(same, even)
        ds = [jnp.where(keep, m, 0.0) + odd_one for m in tiles]
        if b > 1:
            xs = inverse(ds, 1.0 + b, one128)
        else:
            xs = [jnp.where(keep, 1.0 / d, 0.0) + odd_one for d in
                  [jnp.where(i == j, dd, 1.0) for dd in ds]]
        gs = [dot3(lo, x) for lo, x in zip(lows, xs)]
        tiles = [jnp.where(same, m, 0.0) - dot3(g, lo, NT) for m, g, lo in zip(tiles, gs, lows)]
        if ts is None:
            ts = [one128 - g for g in gs]
        else:
            ts = [t - dot3(g, t) for t, g in zip(ts, gs)]
        b //= 2
    ts = [lax.rsqrt(jnp.sum(jnp.where(i == j, m, 0.0), axis=1, keepdims=True)) * t
          for m, t in zip(tiles, ts)]
    zero = jnp.zeros((128, 128), F32)
    hs = []
    for k in range(2):
        hs.append(jnp.concatenate([
            jnp.concatenate([ts[2 * k], zero], 1),
            jnp.concatenate([-dot3(ts[2 * k + 1], g2[k]), ts[2 * k + 1]], 1)], 0))
    w11, w22 = hs
    w21 = -jnp.concatenate([dot3(ts[2], g1p[:128]), dot3(ts[3], g1p[128:])], 0)
    i, j = tri_low(256)
    low_half = jnp.where(i > j, 1.0, jnp.where(i == j, 0.5, 0.0))
    a_s = split(a_ref[...])

    def cut(p, r, c):
        return p[0][r, c], p[1][r, c]
    lo, hi, al = slice(0, 256), slice(256, 512), slice(0, 512)
    for _ in range(2):
        w1s = split(w11)
        w2s = split(jnp.concatenate([w21, w22], 1))
        wa1 = split(dot3s(w1s, cut(a_s, lo, lo)))
        wa2 = split(dot3s(w2s, a_s))
        e11 = (dot3s(wa1, w1s, NT) - one256) * low_half
        e21 = dot3s(cut(wa2, al, lo), w1s, NT)
        e22 = (dot3s(wa2, w2s, NT) - one256) * low_half
        p11, p21, p22 = e11.astype(BF16), e21.astype(BF16), e22.astype(BF16)
        w11 = w11 - mm(p11, w1s[0], NN)
        nw2 = mm(p22, w2s[0], NN)
        w21 = w21 - nw2[:, :256] - mm(p21, w1s[0], NN)
        w22 = w22 - nw2[:, 256:]
    w_ref[0:256, 0:256] = w11
    w_ref[0:256, 256:512] = jnp.zeros((256, 256), F32)
    w_ref[256:512, 0:256] = w21
    w_ref[256:512, 256:512] = w22

    w_s = split(w_ref[...])
    d = row * COLS + z
    base = d // 4
    l_ref[...] = dot3s(split(a_ref[pl.ds(pl.multiple_of(base * 8, 8), 8), :]), w_s, NT)
    lane = lax.broadcasted_iota(jnp.int32, (1, 512), 1)
    for s in range(2):
        line = l_ref[pl.ds(2 * (d % 4) + s, 1), :]
        line = jnp.where(lane <= 2 * d + s, line, 0.0)
        for l in range(4):
            fd_ref[2 * l + s:2 * l + s + 1, :] = line[:, l * 128:(l + 1) * 128]

    b_t = br_ref[...]
    fp_ref[...] = dot3(w_ref[pl.ds(pl.multiple_of(z * 64, 64), 64), :], b_t)
    p_r = dot3s(split(b_t.T), w_s, NT)
    u_s = split(dot3s(split(p_r), w_s))
    for q in range(4):
        cols = slice(q * 256, (q + 1) * 256)
        s_ref[:, cols] = t_ref[:, cols] - dot3s(u_s, split(bc_ref[q]))


def factor(g, br, bc, trailing):
    vmem = pl.BlockSpec(memory_space=pltpu.VMEM)
    return pl.pallas_call(
        factor_kernel,
        out_shape=(
            jax.ShapeDtypeStruct((8, 128), F32),
            jax.ShapeDtypeStruct((64, 256), F32),
            jax.ShapeDtypeStruct((256, 1024), F32),
        ),
        in_specs=[vmem] * 4,
        out_specs=(vmem,) * 3,
        scratch_shapes=[
            pltpu.VMEM((4, 512, 128), F32),
            pltpu.VMEM((512, 512), F32),
            pltpu.VMEM((512, 512), F32),
            pltpu.VMEM((8, 512), F32),
        ],
        compiler_params=pltpu.CompilerParams(vmem_limit_bytes=60 * 1024 * 1024),
        name="factor",
    )(g, br, bc, trailing)


def per_device(diag_block, panel_block, trailing):
    tile = diag_block.reshape(2, 4, 128).transpose(1, 0, 2).reshape(8, 128)
    g, br, bc = gather(tile, panel_block.T)
    fd, fp, schur = factor(
        g.reshape(2048, 128), br.reshape(512, 256), bc.reshape(4, 512, 256), trailing)
    fd = fd.reshape(4, 2, 128).transpose(1, 0, 2).reshape(2, 512)
    return fd, fp.T, schur


def solution(mesh):
    return jax.shard_map(
        per_device,
        mesh=mesh,
        in_specs=(P(("row", "col"), None), P("row", "col"), P("row", "col")),
        out_specs=(P(("row", "col"), None), P("row", "col"), P("row", "col")),
        check_vma=False,
    )
```

time: 355 us -> 66.2 us (0.19)
  waiting for transfers between devices: 168 us -> 0 us
  other arithmetic: 119 us -> 0 us
  Pallas kernels: 0 us -> 65.4 us
  blocking collectives: 26.5 us -> 0 us
  between operations: 16.9 us -> 0.64 us
  matrix products: 12.3 us -> 0 us
  local copies, waits for them, and re-layouts: 11.6 us -> 0 us
    all_gather x2 -> x0, waiting for transfers between devices: 167 us -> none  [the longest x1 84.4 us: per_device(): gathered = lax.all_gather(diag_block, ('row', 'col'), axis=0, tiled=True)]
    another operation x17 -> x0, other arithmetic: 118 us -> none  [the longest x14 78.7 us: per_device(): factor = jnp.linalg.cholesky(gathered)]
    pallas_call x0 -> x2, Pallas kernels: none -> 65.4 us  [the longest x1 42 us: gather(): pl.pallas_call(gather_kernel, out_shape=(jax.ShapeDtypeStruct((CHIPS, 2,...]
    all_gather x1 -> x0, blocking collectives: 26.5 us -> none  [per_device(): full_rows = lax.all_gather(panel_block, 'col', axis=1, tiled=True)]
    another operation x17 -> x0, local copies, waits for them, and re-layouts: 8.07 us -> none
    another operation x13 -> x0, matrix products: 7.65 us -> none  [the longest x7 5.78 us: forward(): return jax.scipy.linalg.solve_triangular(factor, rows_in.T, lower=True).T]
    dot_general x1 -> x0, matrix products: 4.7 us -> none  [per_device(): lax.dot_general(solved, column_factor, (((1,), (1,)), ((), ())), precisio...]
  transfers between devices with their start and end apart: 2 -> 0, of which waited for: 2 -> 0; matrix products, arithmetic and copies ran while one was open for 0% -> 0% of each run, Pallas kernels for 0% -> 0%
where the time goes in v1:
time: 66.2 us; the launch traced here: 66 us
  Pallas kernels  65.4 us (99%)
    pallas_call x1, Pallas kernels, gather(): pl.pallas_call(gather_kernel, out_shape=(jax.ShapeDtypeStruct((CHIPS, 2,...  42 us
    pallas_call x1, Pallas kernels, factor(): pl.pallas_call(factor_kernel, out_shape=(jax.ShapeDtypeStruct((8, 128), F...  23.4 us

profile of v1, /device:TPU:1, one launch (start us, length us, event | category | flops | bytes accessed | tf_op | source)
XLA Modules:
  0.0 66.0 jit_solution(1777168076471905375)
XLA Ops:
  0.6 42.0 %gather.1 = (f32[16,2,8,8,128]{4,3,2,1,0:T(8,128)}, f32[8,64,256]{2,1,0:T(8,128)}, f32[2,2,8,64,256]{4,3,2,1,0:T(8,128)}) custom-call(f32[8,128]{1,0:T(8,128)} %bitcast.19, f32[64,256]{1,0:T(8,128)} %bitcast.18), custom_call_target="tpu_custom_call" | custom-call | tf_op jit(solution)/shard_map/gather/pallas_call | solution.py:136
  42.7 23.4 %factor.1 = (f32[8,128]{1,0:T(8,128)}, f32[64,256]{1,0:T(8,128)}, f32[256,1024]{1,0:T(8,128)}) custom-call(f32[2048,128]{1,0:T(8,128)} %bitcast.16, f32[512,256]{1,0:T(8,128)} %bitcast.17, f32[4,512,256]{2,1,0:T(8,128)} %bitcast.15, f32[256,1024]{1,0:T(8,128)} %t_ref.1), custom_call_target="tpu_custom_call" | custom-call | tf_op jit(solution)/shard_map/factor/pallas_call | solution.py:327

commit v2 on v0

v2 whole, which is shorter than its diff:
```python
import functools

import jax
import jax.numpy as jnp
from jax import lax
from jax.experimental import pallas as pl
from jax.experimental.pallas import tpu as pltpu
from jax.sharding import PartitionSpec as P

NB = 512
F32 = jnp.float32
BF16 = jnp.bfloat16
MESH = pl.DeviceIdType.MESH
CHIPS = 16
COLS = 8


def split(x):
    high = x.astype(BF16)
    return high, (x - high.astype(F32)).astype(BF16)


def mm(a, b, dims):
    return lax.dot_general(a, b, (dims, ((), ())), preferred_element_type=F32)


NN = ((1,), (0,))
NT = ((1,), (1,))


def dot3s(a, b, dims=NN):
    return mm(a[0], b[0], dims) + (mm(a[0], b[1], dims) + mm(a[1], b[0], dims))


def dot3(a, b, dims=NN):
    return dot3s(split(a), split(b), dims)


def dotp(a, b):
    bh, bl = split(b)
    w = jnp.concatenate([bh, bl], 1)
    out = mm(jnp.concatenate(split(a), 1), jnp.concatenate([w, w], 0), NN)
    n = b.shape[1]
    return out[:, :n] + out[:, n:]


def dotp_t(a, b):
    bh, bl = split(b)
    w = jnp.concatenate([jnp.concatenate([bh, bh], 1), jnp.concatenate([bl, bl], 1)], 0)
    out = mm(jnp.concatenate(split(a), 1), w, NT)
    n = b.shape[0]
    return out[:, :n] + out[:, n:]


def scales(top, tol):
    e = (top - 1.0) / (top + 1.0)
    out = []
    while e > tol:
        m = 2.0 / (2.0 - e * e)
        out.append(m)
        e = e * e * m / 2.0
    return 2.0 / (1.0 + top), out


def grid2(n):
    i = lax.broadcasted_iota(jnp.int32, (n, n), 0)
    j = lax.broadcasted_iota(jnp.int32, (n, n), 1)
    return i, j


TOL = {256: 3e-4, 128: 1e-3, 64: 1e-3, 32: 1e-3, 16: 1e-3}
BASE = 16


def half_split(m, n, dot, dot_t):
    i, j = grid2(n)
    start, steps = scales(1.0 + n, TOL[n])
    zs = [start * x[:, :n] for x in m]
    for k, s in enumerate(steps):
        ns = [jnp.where(i == j, 2.0 * s, 0.0) - s * z[:n] for z in zs]
        if k == len(steps) - 1:
            zs = [z[n:] for z in zs]
        zs = [dot(z, nn) for z, nn in zip(zs, ns)]
    return zs, [x[n:, n:] - dot_t(z, x[n:, :n]) for x, z in zip(m, zs)]


def base_factors(tiles):
    sub = lax.broadcasted_iota(jnp.int32, (BASE, 128), 0)
    lane = lax.broadcasted_iota(jnp.int32, (BASE, 128), 1)
    groups = 128 // BASE
    rows = []
    for m in tiles:
        acc = None
        for g in range(groups):
            part = jnp.where(lane // BASE == g, m[g * BASE:(g + 1) * BASE], 0.0)
            acc = part if acc is None else acc + part
        rows.append(acc)
    ident = jnp.where(sub == lane % BASE, 1.0, 0.0)
    es = [ident] * len(tiles)
    for p in range(BASE):
        index = (lane // BASE) * BASE + p
        for t in range(len(tiles)):
            col = jnp.take_along_axis(rows[t], index, axis=1, mode="promise_in_bounds")
            root = lax.rsqrt(col[p:p + 1])
            e_row = es[t][p:p + 1] * root
            if p < BASE - 1:
                a_row = rows[t][p:p + 1] * (root * root)
                below = jnp.where(sub > p, col, 0.0)
                rows[t] = rows[t] - below * a_row
                es[t] = jnp.where(sub == p, e_row, es[t] - below * (e_row * root))
            else:
                es[t] = jnp.where(sub == p, e_row, es[t])
    return [jnp.concatenate([jnp.where(lane // BASE == g, e, 0.0) for g in range(groups)], 0)
            for e in es]


def factor_inverse(a, between=lambda: None):
    (g1,), (s,) = half_split([a[...]], 256, dot3, lambda x, y: dot3(x, y, NT))
    blocks = [a[0:256, 0:256], s]
    g2, s2 = half_split(blocks, 128, dotp, dotp_t)
    tiles = [blocks[0][:128, :128], s2[0], blocks[1][:128, :128], s2[1]]
    i, j = grid2(128)
    ts = None
    b = 64
    while b >= BASE:
        bi, bj = i // b, j // b
        start, steps = scales(1.0 + b, TOL[b])
        pair = jnp.logical_and(i // (2 * b) == j // (2 * b), bj % 2 == 0)
        even = bi % 2 == 0
        low = jnp.logical_and(pair, jnp.logical_not(even))
        diag = jnp.logical_and(i == j, even)
        lows = [jnp.where(low, m, 0.0) for m in tiles]
        zs = [jnp.where(pair, start * m, 0.0) for m in tiles]
        for sc in steps:
            ns = [jnp.where(diag, 2.0 * sc, 0.0) - jnp.where(even, sc * z, 0.0) for z in zs]
            zs = [dotp(z, nn) for z, nn in zip(zs, ns)]
        gs = [jnp.where(even, 0.0, z) for z in zs]
        tiles = [jnp.where(bi == bj, m, 0.0) - dotp_t(g, lo) for m, g, lo in zip(tiles, gs, lows)]
        if ts is None:
            ts = [jnp.where(i == j, 1.0, 0.0) - g for g in gs]
        else:
            ts = [t - dotp(g, t) for t, g in zip(ts, gs)]
        b //= 2
    g1p = jnp.concatenate([g1[:128], g1[128:] - dotp(g2[1], g1[:128])], 0)
    bases = base_factors(tiles)
    between()
    ts = [dotp(e, t) for e, t in zip(bases, ts)]
    zero = jnp.zeros((128, 128), F32)
    w11, w22 = [jnp.concatenate([
        jnp.concatenate([ts[2 * k], zero], 1),
        jnp.concatenate([-dotp(ts[2 * k + 1], g2[k]), ts[2 * k + 1]], 1)], 0) for k in range(2)]
    w21 = -jnp.concatenate([dotp(ts[2], g1p[:128]), dotp(ts[3], g1p[128:])], 0)

    i, j = grid2(256)
    one = jnp.where(i == j, 1.0, 0.0)
    low_half = jnp.where(i > j, 1.0, jnp.where(i == j, 0.5, 0.0))
    a_s = split(a[...])
    w1s = split(w11)
    w2s = split(jnp.concatenate([w21, w22], 1))
    wa1 = split(dot3s(w1s, [x[:256, :256] for x in a_s]))
    wa2 = split(dot3s(w2s, a_s))
    p11 = ((dot3s(wa1, w1s, NT) - one) * low_half).astype(BF16)
    p21 = dot3s([x[:, :256] for x in wa2], w1s, NT).astype(BF16)
    p22 = ((dot3s(wa2, w2s, NT) - one) * low_half).astype(BF16)
    n11 = w11 - mm(p11, w1s[0], NN)
    nw2 = mm(p22, w2s[0], NN)
    return n11, w21 - nw2[:, :256] - mm(p21, w1s[0], NN), w22 - nw2[:, 256:]


def step_kernel(d_ref, b_ref, bc_ref, fd_ref, fp_ref, uh_ref, ul_ref,
                g_ref, br_ref, m_ref, a4_ref, a_ref, w_ref, l_ref, bt_ref,
                as_sem, ar_sem, rs_sem, rr_sem, ms_sem, mr_sem, ps_sem, pr_sem, loc_sem):
    row = lax.axis_index("row")
    z = lax.axis_index("col")
    chip = row // 2
    core = row % 2

    def at_z(k):
        return {"row": row, "col": (z + k) % COLS}

    def at_chip(k):
        return {"row": ((chip + k) % CHIPS) * 2 + core, "col": z}

    partner = {"row": row + 1 - 2 * core, "col": z}

    def copy(src, dst, ssem, rsem, device):
        return pltpu.make_async_remote_copy(
            src_ref=src, dst_ref=dst, send_sem=ssem, recv_sem=rsem,
            device_id=device, device_id_type=MESH)

    barrier = pltpu.get_barrier_semaphore()
    for k in range(1, COLS):
        pl.semaphore_signal(barrier, inc=1, device_id=at_z(k), device_id_type=MESH)
    for k in range(1, CHIPS):
        pl.semaphore_signal(barrier, inc=1, device_id=at_chip(k), device_id_type=MESH)
    pl.semaphore_signal(barrier, inc=1, device_id=partner, device_id_type=MESH)
    def tile(c, k, zz):
        first = pl.multiple_of(((c * 2 + k) * COLS + zz) * 8, 8)
        return g_ref.at[pl.ds(first, 8)]

    own_a = pltpu.make_async_copy(d_ref, tile(chip, core, z), loc_sem.at[0])
    own_b = pltpu.make_async_copy(b_ref, br_ref.at[z], loc_sem.at[1])
    own_a.start()
    own_b.start()
    pl.semaphore_wait(barrier, COLS + CHIPS - 1)

    a_z = [copy(d_ref, tile(chip, core, z), as_sem.at[k - 1], ar_sem.at[k - 1], at_z(k))
           for k in range(1, COLS)]
    for c in a_z:
        c.start()

    move1 = copy(b_ref, m_ref, ms_sem.at[0], mr_sem.at[0], at_chip(2 * z))
    move1_own = pltpu.make_async_copy(b_ref, m_ref, loc_sem.at[2])

    @pl.when(z != 0)
    def _():
        move1.start()

    @pl.when(z == 0)
    def _():
        move1_own.start()

    own_a.wait()
    for c in a_z:
        c.wait()

    def line(c):
        return g_ref.at[pl.ds(pl.multiple_of((c * 2 + core) * COLS * 8, 64), 64)]

    a_p = [copy(line(chip), line(chip), as_sem.at[6 + k], ar_sem.at[6 + k], at_chip(k))
           for k in range(1, CHIPS)]
    for c in a_p:
        c.start()

    @pl.when(z != 0)
    def _():
        move1.wait()

    @pl.when(z == 0)
    def _():
        move1_own.wait()

    src = (chip + CHIPS - 2 * z) % CHIPS
    plane = src // 2
    slot = bc_ref.at[src % 2, core, z]
    move2 = copy(m_ref, slot, ms_sem.at[1], mr_sem.at[1], {"row": row, "col": plane})
    move2_own = pltpu.make_async_copy(m_ref, slot, loc_sem.at[3])

    @pl.when(plane != z)
    def _():
        move2.start()

    @pl.when(plane == z)
    def _():
        move2_own.start()

    b_z = [copy(b_ref, br_ref.at[z], rs_sem.at[k - 1], rr_sem.at[k - 1], at_z(k))
           for k in range(1, COLS)]
    for c in b_z:
        c.start()

    a_c = []
    for k in range(CHIPS):
        c = (chip + CHIPS - k) % CHIPS
        if k:
            a_p[k - 1].wait_recv()
        a_c.append(copy(line(c), line(c), as_sem.at[22 + k], ar_sem.at[22 + k], partner))
        a_c[-1].start()
    for c in a_p:
        c.wait_send()

    @pl.when(plane != z)
    def _():
        move2.wait()

    @pl.when(plane == z)
    def _():
        move2_own.wait()

    held = bc_ref.at[chip % 2, core, (chip // 2 + COLS - z) % COLS]
    b_p = [copy(held, held, ps_sem.at[k - 1], pr_sem.at[k - 1], at_chip(k))
           for k in range(1, CHIPS)]
    for c in b_p:
        c.start()
    for c in a_c:
        c.wait()

    for s in range(2):
        for l in range(4):
            a4_ref[l, pl.ds(s, 256, stride=2), :] = (
                g_ref[pl.ds(2 * l + s, 256, stride=8), :])
    for l in range(4):
        a_ref[:, l * 128:(l + 1) * 128] = a4_ref[l]

    bhalf = bc_ref.at[:, core]
    b_c = copy(bhalf, bhalf, ps_sem.at[15], pr_sem.at[15], partner)

    def between():
        own_b.wait()
        for c in b_z:
            c.wait()
        bt_ref[...] = br_ref[...].reshape(512, 256).T
        for c in b_p:
            c.wait()
        b_c.start()

    w11, w21, w22 = factor_inverse(a_ref, between)
    w_ref[0:256, 0:256] = w11
    w_ref[0:256, 256:512] = jnp.zeros((256, 256), F32)
    w_ref[256:512, 0:256] = w21
    w_ref[256:512, 256:512] = w22

    w1s = split(w11)
    w2s = split(jnp.concatenate([w21, w22], 1))
    d = row * COLS + z
    mine = split(a_ref[pl.ds(pl.multiple_of((d // 4) * 8, 8), 8), :])
    l_ref[:, 0:256] = dot3s([x[:, :256] for x in mine], w1s, NT)
    l_ref[:, 256:512] = dot3s(mine, w2s, NT)
    lane = lax.broadcasted_iota(jnp.int32, (1, 512), 1)
    for s in range(2):
        line_s = l_ref[pl.ds(2 * (d % 4) + s, 1), :]
        line_s = jnp.where(lane <= 2 * d + s, line_s, 0.0)
        for l in range(4):
            fd_ref[2 * l + s:2 * l + s + 1, :] = line_s[:, l * 128:(l + 1) * 128]

    fp_ref[...] = dot3(w_ref[pl.ds(pl.multiple_of(z * 64, 64), 64), :],
                       br_ref[...].reshape(512, 256))
    b_s = split(bt_ref[...])
    p1 = split(dot3s([x[:, :256] for x in b_s], w1s, NT))
    p2 = split(dot3s(b_s, w2s, NT))
    u2 = dot3s(p2, w2s)
    u1 = u2[:, :256] + dot3s(p1, w1s)
    for cols, u in ((slice(0, 256), u1), (slice(256, 512), u2[:, 256:])):
        uh_ref[:, cols], ul_ref[:, cols] = split(u)
    b_c.wait()


def step(d_tile, b_t):
    vmem = pl.BlockSpec(memory_space=pltpu.VMEM)
    dma = pltpu.SemaphoreType.DMA
    return pl.pallas_call(
        step_kernel,
        out_shape=(
            jax.ShapeDtypeStruct((2, 2, COLS, 64, 256), F32),
            jax.ShapeDtypeStruct((8, 128), F32),
            jax.ShapeDtypeStruct((64, 256), F32),
            jax.ShapeDtypeStruct((256, 512), BF16),
            jax.ShapeDtypeStruct((256, 512), BF16),
        ),
        in_specs=[vmem] * 2,
        out_specs=(pl.BlockSpec(memory_space=pl.ANY),) + (vmem,) * 4,
        scratch_shapes=[
            pltpu.VMEM((2048, 128), F32),
            pltpu.VMEM((COLS, 64, 256), F32),
            pltpu.VMEM((64, 256), F32),
            pltpu.VMEM((4, 512, 128), F32),
            pltpu.VMEM((512, 512), F32),
            pltpu.VMEM((512, 512), F32),
            pltpu.VMEM((8, 512), F32),
            pltpu.VMEM((256, 512), F32),
            dma((38,)), dma((38,)), dma((7,)), dma((7,)), dma((2,)), dma((2,)),
            dma((16,)), dma((16,)), dma((4,)),
        ],
        compiler_params=pltpu.CompilerParams(
            collective_id=0, has_side_effects=True, vmem_limit_bytes=40 * 1024 * 1024),
        name="step",
    )(d_tile, b_t)


def update_kernel(uh_ref, ul_ref, bc_ref, t_ref, fd_in, fp_in, s_ref, fd_ref, fp_ref):
    s_ref[...] = t_ref[...] - dot3s((uh_ref[...], ul_ref[...]), split(bc_ref[...]))

    @pl.when(pl.program_id(0) == 0)
    def _():
        fd_ref[...] = fd_in[...]
        fp_ref[...] = fp_in[...]


def update(uh, ul, bc, trailing, fd, fp):
    whole = lambda shape: pl.BlockSpec(shape, lambda q: (0, 0))
    block = pl.BlockSpec((256, 256), lambda q: (0, q))
    return pl.pallas_call(
        update_kernel,
        grid=(4,),
        out_shape=(
            jax.ShapeDtypeStruct((256, 1024), F32),
            jax.ShapeDtypeStruct((8, 128), F32),
            jax.ShapeDtypeStruct((64, 256), F32),
        ),
        in_specs=[whole((256, 512)), whole((256, 512)),
                  pl.BlockSpec((None, 512, 256), lambda q: (q, 0, 0)), block,
                  whole((8, 128)), whole((64, 256))],
        out_specs=(block, whole((8, 128)), whole((64, 256))),
        compiler_params=pltpu.CompilerParams(vmem_limit_bytes=16 * 1024 * 1024),
        name="update",
    )(uh, ul, bc, trailing, fd, fp)


def per_device(diag_block, panel_block, trailing):
    tile = diag_block.reshape(2, 4, 128).transpose(1, 0, 2).reshape(8, 128)
    bc, fd, fp, uh, ul = step(tile, panel_block.T)
    schur, fd, fp = update(uh, ul, bc.reshape(4, 512, 256), trailing, fd, fp)
    fd = fd.reshape(4, 2, 128).transpose(1, 0, 2).reshape(2, 512)
    return fd, fp.T, schur


def solution(mesh):
    return jax.shard_map(
        per_device,
        mesh=mesh,
        in_specs=(P(("row", "col"), None), P("row", "col"), P("row", "col")),
        out_specs=(P(("row", "col"), None), P("row", "col"), P("row", "col")),
        check_vma=False,
    )
```

time: 355 us -> 46.8 us (0.13)
  waiting for transfers between devices: 168 us -> 0 us
  other arithmetic: 119 us -> 0 us
  Pallas kernels: 0 us -> 43.2 us
  blocking collectives: 26.5 us -> 0 us
  between operations: 16.9 us -> 0.66 us
  matrix products: 12.3 us -> 0 us
  local copies, waits for them, and re-layouts: 11.6 us -> 2.74 us
    all_gather x2 -> x0, waiting for transfers between devices: 167 us -> none  [the longest x1 84.4 us: per_device(): gathered = lax.all_gather(diag_block, ('row', 'col'), axis=0, tiled=True)]
    another operation x17 -> x0, other arithmetic: 118 us -> none  [the longest x14 78.7 us: per_device(): factor = jnp.linalg.cholesky(gathered)]
    pallas_call x0 -> x2, Pallas kernels: none -> 43.2 us  [the longest x1 40.5 us: step(): pl.pallas_call(step_kernel, out_shape=(jax.ShapeDtypeStruct((2, 2, COLS,...]
    all_gather x1 -> x0, blocking collectives: 26.5 us -> none  [per_device(): full_rows = lax.all_gather(panel_block, 'col', axis=1, tiled=True)]
    another operation x17 -> x0, local copies, waits for them, and re-layouts: 8.07 us -> none
    another operation x13 -> x0, matrix products: 7.65 us -> none  [the longest x7 5.78 us: forward(): return jax.scipy.linalg.solve_triangular(factor, rows_in.T, lower=True).T]
    dot_general x1 -> x0, matrix products: 4.7 us -> none  [per_device(): lax.dot_general(solved, column_factor, (((1,), (1,)), ((), ())), precisio...]
  transfers between devices with their start and end apart: 2 -> 0, of which waited for: 2 -> 0; matrix products, arithmetic and copies ran while one was open for 0% -> 0% of each run, Pallas kernels for 0% -> 0%
where the time goes in v2:
time: 46.8 us; the launch traced here: 46.6 us
  Pallas kernels  43.2 us (92%)
  local copies, waits for them, and re-layouts  2.74 us (6%)
  between operations  0.66 us (1%)
    pallas_call x1, Pallas kernels, step(): pl.pallas_call(step_kernel, out_shape=(jax.ShapeDtypeStruct((2, 2, COLS,...  40.5 us
    unnamed x6, local copies, waits for them, and re-layouts  2.74 us
    pallas_call x1, Pallas kernels, update(): pl.pallas_call(update_kernel, grid=(4,), out_shape=(jax.ShapeDtypeStruct(...  2.68 us

profile of v2, /device:TPU:1, one launch (start us, length us, event | category | flops | bytes accessed | tf_op | source)
XLA Modules:
  0.0 46.6 jit_solution(16370210192932462758)
XLA Ops:
  0.6 0.0 copy-start.1
  0.6 0.8 %copy-done.1 = f32[256,64]{0,1:T(8,128)S(1)} copy-done((f32[256,64]{0,1:T(8,128)S(1)}, f32[256,64]{0,1:T(8,128)}, u32[]{:S(2)}) %copy-start.1) | copy-done | bytes 65560
  1.5 0.0 copy-start.2
  1.5 0.7 %copy-done.2 = f32[2,512]{1,0:T(2,128)S(1)} copy-done((f32[2,512]{1,0:T(2,128)S(1)}, f32[2,512]{1,0:T(2,128)}, u32[]{:S(2)}) %copy-start.2) | copy-done | bytes 4120
  2.2 40.5 %step.1 = (f32[2,2,8,64,256]{4,3,2,1,0:T(8,128)S(1)}, f32[8,128]{1,0:T(8,128)S(1)}, f32[64,256]{1,0:T(8,128)S(1)}, bf16[256,512]{1,0:T(8,128)(2,1)S(1)}, bf16[256,512]{1,0:T(8,128)(2,1)S(1)}) custom-call(f32[8,128]{1,0:T(8,128)S(1)} %bitcast.15, f32[64,256]{1,0:T(8,128)S(1)} %bitcast.14), custom_call_target="tpu_custom_call" | custom-call | tf_op jit(solution)/shard_map/step/pallas_call | solution.py:341
  42.7 0.0 copy-start
  42.7 1.2 %copy-done = f32[256,1024]{1,0:T(8,128)S(1)} copy-done((f32[256,1024]{1,0:T(8,128)S(1)}, f32[256,1024]{1,0:T(8,128)}, u32[]{:S(2)}) %copy-start) | copy-done | bytes 1048600
  43.9 2.7 %update.1 = (f32[256,1024]{1,0:T(8,128)}, f32[8,128]{1,0:T(8,128)}, f32[64,256]{1,0:T(8,128)}) custom-call(bf16[256,512]{1,0:T(8,128)(2,1)S(1)} %get-tuple-element.11.uh_ref, bf16[256,512]{1,0:T(8,128)(2,1)S(1)} %get-tuple-element.12.ul_ref, f32[4,512,256]{2,1,0:T(8,128)S(1)} %bitcast.13, f32[256,1024]{1,0:T(8,128)S(1)} %copy-done, ...), custom_call_target="tpu_custom_call" | custom-call | tf_op jit(solution)/shard_map/update/pallas_call | solution.py:382
Async XLA Ops:
  0.6 0.8 %copy-start.1 = (f32[256,64]{0,1:T(8,128)S(1)}, f32[256,64]{0,1:T(8,128)}, u32[]{:S(2)}) copy-start(f32[256,64]{0,1:T(8,128)} %param.4) | copy-start | bytes 196612
  1.5 0.7 %copy-start.2 = (f32[2,512]{1,0:T(2,128)S(1)}, f32[2,512]{1,0:T(2,128)}, u32[]{:S(2)}) copy-start(f32[2,512]{1,0:T(2,128)} %param.3) | copy-start | bytes 12292
  42.7 1.2 %copy-start = (f32[256,1024]{1,0:T(8,128)S(1)}, f32[256,1024]{1,0:T(8,128)}, u32[]{:S(2)}) copy-start(f32[256,1024]{1,0:T(8,128)} %t_ref.1) | copy-start | bytes 3145732

commit v3 on v2

--- a/solution.py
+++ b/solution.py
@@ -167,19 +167,28 @@
     return n11, w21 - nw2[:, :256] - mm(p21, w1s[0], NN), w22 - nw2[:, 256:]
 
 
-def step_kernel(d_ref, b_ref, bc_ref, fd_ref, fp_ref, uh_ref, ul_ref,
+def step_kernel(d_ref, b_ref, t_ref, bc_ref, fd_ref, fp_ref, uh_ref, ul_ref, to_ref,
                 g_ref, br_ref, m_ref, a4_ref, a_ref, w_ref, l_ref, bt_ref,
-                as_sem, ar_sem, rs_sem, rr_sem, ms_sem, mr_sem, ps_sem, pr_sem, loc_sem):
+                az_s, az_r, ax_s, ax_r, ay_s, ay_r, ac_s, ac_r,
+                bz_s, bz_r, mv_s, mv_r, bx_s, bx_r, by_s, by_r, bk_s, bk_r, loc_sem):
     row = lax.axis_index("row")
     z = lax.axis_index("col")
     chip = row // 2
     core = row % 2
+    y = chip // 4
+    x = chip % 4
 
     def at_z(k):
         return {"row": row, "col": (z + k) % COLS}
 
     def at_chip(k):
         return {"row": ((chip + k) % CHIPS) * 2 + core, "col": z}
+
+    def at_x(k):
+        return {"row": (y * 4 + (x + k) % 4) * 2 + core, "col": z}
+
+    def at_y(k):
+        return {"row": (((y + k) % 4) * 4 + x) * 2 + core, "col": z}
 
     partner = {"row": row + 1 - 2 * core, "col": z}
 
@@ -187,6 +196,10 @@
         return pltpu.make_async_remote_copy(
             src_ref=src, dst_ref=dst, send_sem=ssem, recv_sem=rsem,
             device_id=device, device_id_type=MESH)
+
+    def fan(ref, ssem, rsem, first, where, n):
+        return [copy(ref, ref, ssem.at[first + k - 1], rsem.at[first + k - 1], where(k))
+                for k in range(1, n + 1)]
 
     barrier = pltpu.get_barrier_semaphore()
     for k in range(1, COLS):
@@ -194,22 +207,20 @@
     for k in range(1, CHIPS):
         pl.semaphore_signal(barrier, inc=1, device_id=at_chip(k), device_id_type=MESH)
     pl.semaphore_signal(barrier, inc=1, device_id=partner, device_id_type=MESH)
-    def tile(c, k, zz):
-        first = pl.multiple_of(((c * 2 + k) * COLS + zz) * 8, 8)
-        return g_ref.at[pl.ds(first, 8)]
-
-    own_a = pltpu.make_async_copy(d_ref, tile(chip, core, z), loc_sem.at[0])
+    own_tile = g_ref.at[y, x, core, z]
+    own_a = pltpu.make_async_copy(d_ref, own_tile, loc_sem.at[0])
     own_b = pltpu.make_async_copy(b_ref, br_ref.at[z], loc_sem.at[1])
+    own_t = pltpu.make_async_copy(t_ref, to_ref, loc_sem.at[4])
     own_a.start()
     own_b.start()
     pl.semaphore_wait(barrier, COLS + CHIPS - 1)
 
-    a_z = [copy(d_ref, tile(chip, core, z), as_sem.at[k - 1], ar_sem.at[k - 1], at_z(k))
+    a_z = [copy(d_ref, own_tile, az_s.at[k - 1], az_r.at[k - 1], at_z(k))
            for k in range(1, COLS)]
     for c in a_z:
         c.start()
 
-    move1 = copy(b_ref, m_ref, ms_sem.at[0], mr_sem.at[0], at_chip(2 * z))
+    move1 = copy(b_ref, m_ref, mv_s.at[0], mv_r.at[0], at_chip(2 * z))
     move1_own = pltpu.make_async_copy(b_ref, m_ref, loc_sem.at[2])
 
     @pl.when(z != 0)
@@ -220,17 +231,17 @@
     def _():
         move1_own.start()
 
+    own_t.start()
     own_a.wait()
     for c in a_z:
         c.wait()
 
-    def line(c):
-        return g_ref.at[pl.ds(pl.multiple_of((c * 2 + core) * COLS * 8, 64), 64)]
-
-    a_p = [copy(line(chip), line(chip), as_sem.at[6 + k], ar_sem.at[6 + k], at_chip(k))
-           for k in range(1, CHIPS)]
-    for c in a_p:
-        c.start()
+    lo, hi = pl.ds(0, 4), pl.ds(4, 4)
+    a_x = fan(g_ref.at[y, x, core, lo], ax_s, ax_r, 0, at_x, 3)
+    a_y = fan(g_ref.at[y, x, core, hi], ay_s, ay_r, 0, at_y, 3)
+    for p, q in zip(a_x, a_y):
+        p.start()
+        q.start()
 
     @pl.when(z != 0)
     def _():
@@ -242,8 +253,8 @@
 
     src = (chip + CHIPS - 2 * z) % CHIPS
     plane = src // 2
-    slot = bc_ref.at[src % 2, core, z]
-    move2 = copy(m_ref, slot, ms_sem.at[1], mr_sem.at[1], {"row": row, "col": plane})
+    slot = bc_ref.at[core, y, x]
+    move2 = copy(m_ref, slot, mv_s.at[1], mv_r.at[1], {"row": row, "col": plane})
     move2_own = pltpu.make_async_copy(m_ref, slot, loc_sem.at[3])
 
     @pl.when(plane != z)
@@ -254,55 +265,88 @@
     def _():
         move2_own.start()
 
-    b_z = [copy(b_ref, br_ref.at[z], rs_sem.at[k - 1], rr_sem.at[k - 1], at_z(k))
+    for c in a_x:
+        c.wait()
+    a_xy = fan(g_ref.at[y, :, core, lo], ay_s, ay_r, 3, at_y, 3)
+    for c in a_xy:
+        c.start()
+    for c in a_y:
+        c.wait()
+    a_yx = fan(g_ref.at[:, x, core, hi], ax_s, ax_r, 3, at_x, 3)
+    for c in a_yx:
+        c.start()
+
+    b_z = [copy(b_ref, br_ref.at[z], bz_s.at[k - 1], bz_r.at[k - 1], at_z(k))
            for k in range(1, COLS)]
     for c in b_z:
         c.start()
 
-    a_c = []
-    for k in range(CHIPS):
-        c = (chip + CHIPS - k) % CHIPS
-        if k:
-            a_p[k - 1].wait_recv()
-        a_c.append(copy(line(c), line(c), as_sem.at[22 + k], ar_sem.at[22 + k], partner))
-        a_c[-1].start()
-    for c in a_p:
+    def to_partner(ref, ssem, rsem, k):
+        c = copy(ref, ref, ssem.at[k], rsem.at[k], partner)
+        c.start()
+        return c
+
+    a_c = [to_partner(g_ref.at[y, :, core, lo], ac_s, ac_r, 0),
+           to_partner(g_ref.at[:, x, core, hi], ac_s, ac_r, 4)]
+
+    @pl.when(plane != z)
+    def _():
+        move2.wait()
+
+    @pl.when(plane == z)
+    def _():
+        move2_own.wait()
+
+    blo, bhi = pl.ds(0, 32), pl.ds(32, 32)
+    b_x = fan(bc_ref.at[core, y, x, blo], bx_s, bx_r, 0, at_x, 3)
+    b_y = fan(bc_ref.at[core, y, x, bhi], by_s, by_r, 0, at_y, 3)
+    for p, q in zip(b_x, b_y):
+        p.start()
+        q.start()
+
+    for k in range(1, 4):
+        a_xy[k - 1].wait_recv()
+        a_c.append(to_partner(g_ref.at[(y + 4 - k) % 4, :, core, lo], ac_s, ac_r, k))
+        a_yx[k - 1].wait_recv()
+        a_c.append(to_partner(g_ref.at[:, (x + 4 - k) % 4, core, hi], ac_s, ac_r, 4 + k))
+    for c in a_xy + a_yx:
         c.wait_send()
 
-    @pl.when(plane != z)
-    def _():
-        move2.wait()
-
-    @pl.when(plane == z)
-    def _():
-        move2_own.wait()
-
-    held = bc_ref.at[chip % 2, core, (chip // 2 + COLS - z) % COLS]
-    b_p = [copy(held, held, ps_sem.at[k - 1], pr_sem.at[k - 1], at_chip(k))
-           for k in range(1, CHIPS)]
-    for c in b_p:
+    for c in b_x:
+        c.wait()
+    b_xy = fan(bc_ref.at[core, y, :, blo], by_s, by_r, 3, at_y, 3)
+    for c in b_xy:
+        c.start()
+    for c in b_y:
+        c.wait()
+    b_yx = fan(bc_ref.at[core, :, x, bhi], bx_s, bx_r, 3, at_x, 3)
+    for c in b_yx:
         c.start()
     for c in a_c:
         c.wait()
 
-    for s in range(2):
-        for l in range(4):
-            a4_ref[l, pl.ds(s, 256, stride=2), :] = (
-                g_ref[pl.ds(2 * l + s, 256, stride=8), :])
+    for r in range(2 * CHIPS):
+        for s in range(2):
+            for l in range(4):
+                a4_ref[l, pl.ds(16 * r + s, 8, stride=2), :] = (
+                    g_ref[r // 8, r // 2 % 4, r % 2, :, 2 * l + s, :])
     for l in range(4):
         a_ref[:, l * 128:(l + 1) * 128] = a4_ref[l]
 
-    bhalf = bc_ref.at[:, core]
-    b_c = copy(bhalf, bhalf, ps_sem.at[15], pr_sem.at[15], partner)
+    b_c = []
 
     def between():
+        b_c.append(to_partner(bc_ref.at[core, y, :, blo], bk_s, bk_r, 0))
+        b_c.append(to_partner(bc_ref.at[core, :, x, bhi], bk_s, bk_r, 4))
         own_b.wait()
         for c in b_z:
             c.wait()
         bt_ref[...] = br_ref[...].reshape(512, 256).T
-        for c in b_p:
-            c.wait()
-        b_c.start()
+        for k in range(1, 4):
+            b_xy[k - 1].wait()
+            b_c.append(to_partner(bc_ref.at[core, (y + 4 - k) % 4, :, blo], bk_s, bk_r, k))
+            b_yx[k - 1].wait()
+            b_c.append(to_partner(bc_ref.at[core, :, (x + 4 - k) % 4, bhi], bk_s, bk_r, 4 + k))
 
     w11, w21, w22 = factor_inverse(a_ref, between)
     w_ref[0:256, 0:256] = w11
@@ -314,7 +358,7 @@
     w2s = split(jnp.concatenate([w21, w22], 1))
     d = row * COLS + z
     mine = split(a_ref[pl.ds(pl.multiple_of((d // 4) * 8, 8), 8), :])
-    l_ref[:, 0:256] = dot3s([x[:, :256] for x in mine], w1s, NT)
+    l_ref[:, 0:256] = dot3s([v[:, :256] for v in mine], w1s, NT)
     l_ref[:, 256:512] = dot3s(mine, w2s, NT)
     lane = lax.broadcasted_iota(jnp.int32, (1, 512), 1)
     for s in range(2):
@@ -326,31 +370,35 @@
     fp_ref[...] = dot3(w_ref[pl.ds(pl.multiple_of(z * 64, 64), 64), :],
                        br_ref[...].reshape(512, 256))
     b_s = split(bt_ref[...])
-    p1 = split(dot3s([x[:, :256] for x in b_s], w1s, NT))
+    p1 = split(dot3s([v[:, :256] for v in b_s], w1s, NT))
     p2 = split(dot3s(b_s, w2s, NT))
     u2 = dot3s(p2, w2s)
     u1 = u2[:, :256] + dot3s(p1, w1s)
     for cols, u in ((slice(0, 256), u1), (slice(256, 512), u2[:, 256:])):
         uh_ref[:, cols], ul_ref[:, cols] = split(u)
-    b_c.wait()
-
-
-def step(d_tile, b_t):
+    own_t.wait()
+    for c in b_c:
+        c.wait()
+
+
+def step(d_tile, b_t, trailing):
     vmem = pl.BlockSpec(memory_space=pltpu.VMEM)
-    dma = pltpu.SemaphoreType.DMA
+    hbm = pl.BlockSpec(memory_space=pltpu.HBM)
+    dma = lambda n: [pltpu.SemaphoreType.DMA((n,))] * 2
     return pl.pallas_call(
         step_kernel,
         out_shape=(
-            jax.ShapeDtypeStruct((2, 2, COLS, 64, 256), F32),
+            jax.ShapeDtypeStruct((2, 4, 4, 64, 256), F32),
             jax.ShapeDtypeStruct((8, 128), F32),
             jax.ShapeDtypeStruct((64, 256), F32),
             jax.ShapeDtypeStruct((256, 512), BF16),
             jax.ShapeDtypeStruct((256, 512), BF16),
+            jax.ShapeDtypeStruct((256, 1024), F32),
         ),
-        in_specs=[vmem] * 2,
-        out_specs=(pl.BlockSpec(memory_space=pl.ANY),) + (vmem,) * 4,
+        in_specs=[hbm] * 3,
+        out_specs=(vmem,) * 6,
         scratch_shapes=[
-            pltpu.VMEM((2048, 128), F32),
+            pltpu.VMEM((4, 4, 2, COLS, 8, 128), F32),
             pltpu.VMEM((COLS, 64, 256), F32),
             pltpu.VMEM((64, 256), F32),
             pltpu.VMEM((4, 512, 128), F32),
@@ -358,39 +406,46 @@
             pltpu.VMEM((512, 512), F32),
             pltpu.VMEM((8, 512), F32),
             pltpu.VMEM((256, 512), F32),
-            dma((38,)), dma((38,)), dma((7,)), dma((7,)), dma((2,)), dma((2,)),
-            dma((16,)), dma((16,)), dma((4,)),
+            *dma(7), *dma(6), *dma(6), *dma(8),
+            *dma(7), *dma(2), *dma(6), *dma(6), *dma(8),
+            pltpu.SemaphoreType.DMA((5,)),
         ],
         compiler_params=pltpu.CompilerParams(
             collective_id=0, has_side_effects=True, vmem_limit_bytes=40 * 1024 * 1024),
         name="step",
-    )(d_tile, b_t)
-
-
-def update_kernel(uh_ref, ul_ref, bc_ref, t_ref, fd_in, fp_in, s_ref, fd_ref, fp_ref):
-    s_ref[...] = t_ref[...] - dot3s((uh_ref[...], ul_ref[...]), split(bc_ref[...]))
-
-    @pl.when(pl.program_id(0) == 0)
-    def _():
-        fd_ref[...] = fd_in[...]
-        fp_ref[...] = fp_in[...]
+    )(*[pltpu.with_memory_space_constraint(v, pltpu.HBM) for v in (d_tile, b_t, trailing)])
+
+
+def update_kernel(uh_ref, ul_ref, bc_ref, t_ref, fd_in, fp_in, s_ref, fd_ref, fp_ref,
+                  out_ref, sem):
+    z = lax.axis_index("col")
+    u_s = (uh_ref[...], ul_ref[...])
+    copies = []
+    for q in range(4):
+        b, core = q // 2, q % 2
+        rows = jnp.concatenate([bc_ref[core, (k + z) % COLS, b] for k in range(COLS)], 0)
+        cols = slice(q * 256, (q + 1) * 256)
+        out_ref[q] = t_ref[:, cols] - dot3s(u_s, split(rows))
+        copies.append(pltpu.make_async_copy(out_ref.at[q], s_ref.at[:, cols], sem.at[q]))
+        copies[-1].start()
+    fd_ref[...] = fd_in[...]
+    fp_ref[...] = fp_in[...]
+    for c in copies:
+        c.wait()
 
 
 def update(uh, ul, bc, trailing, fd, fp):
-    whole = lambda shape: pl.BlockSpec(shape, lambda q: (0, 0))
-    block = pl.BlockSpec((256, 256), lambda q: (0, q))
+    vmem = pl.BlockSpec(memory_space=pltpu.VMEM)
     return pl.pallas_call(
         update_kernel,
-        grid=(4,),
         out_shape=(
             jax.ShapeDtypeStruct((256, 1024), F32),
             jax.ShapeDtypeStruct((8, 128), F32),
             jax.ShapeDtypeStruct((64, 256), F32),
         ),
-        in_specs=[whole((256, 512)), whole((256, 512)),
-                  pl.BlockSpec((None, 512, 256), lambda q: (q, 0, 0)), block,
-                  whole((8, 128)), whole((64, 256))],
-        out_specs=(block, whole((8, 128)), whole((64, 256))),
+        in_specs=[vmem] * 6,
+        out_specs=(pl.BlockSpec(memory_space=pltpu.HBM), vmem, vmem),
+        scratch_shapes=[pltpu.VMEM((4, 256, 256), F32), pltpu.SemaphoreType.DMA((4,))],
         compiler_params=pltpu.CompilerParams(vmem_limit_bytes=16 * 1024 * 1024),
         name="update",
     )(uh, ul, bc, trailing, fd, fp)
@@ -398,8 +453,8 @@
 
 def per_device(diag_block, panel_block, trailing):
     tile = diag_block.reshape(2, 4, 128).transpose(1, 0, 2).reshape(8, 128)
-    bc, fd, fp, uh, ul = step(tile, panel_block.T)
-    schur, fd, fp = update(uh, ul, bc.reshape(4, 512, 256), trailing, fd, fp)
+    bc, fd, fp, uh, ul, t = step(tile, panel_block.T, trailing)
+    schur, fd, fp = update(uh, ul, bc.reshape(2, COLS, 2, 64, 256), t, fd, fp)
     fd = fd.reshape(4, 2, 128).transpose(1, 0, 2).reshape(2, 512)
     return fd, fp.T, schur
 

time: 46.8 us -> 43.9 us (0.938)
  local copies, waits for them, and re-layouts: 2.74 us -> 0 us
    unnamed x6 -> x0, local copies, waits for them, and re-layouts: 2.74 us -> none
where the time goes in v3:
time: 43.9 us; the launch traced here: 43.5 us
  Pallas kernels  42.9 us (98%)
  between operations  0.64 us (1%)
    pallas_call x1, Pallas kernels, step(): pl.pallas_call(step_kernel, out_shape=(jax.ShapeDtypeStruct((2, 4, 4, 64,...  40.3 us
    pallas_call x1, Pallas kernels, update(): pl.pallas_call(update_kernel, out_shape=(jax.ShapeDtypeStruct((256, 1024)...  2.56 us

profile of v3, /device:TPU:1, one launch (start us, length us, event | category | flops | bytes accessed | tf_op | source)
XLA Modules:
  0.0 43.5 jit_solution(10833871287561478477)
XLA Ops:
  0.6 40.3 %step.1 = (f32[2,4,4,64,256]{4,3,2,1,0:T(8,128)S(1)}, f32[8,128]{1,0:T(8,128)S(1)}, f32[64,256]{1,0:T(8,128)S(1)}, bf16[256,512]{1,0:T(8,128)(2,1)S(1)}, bf16[25...) custom-call(f32[8,128]{1,0:T(8,128)} %bitcast.15, f32[64,256]{1,0:T(8,128)} %bitcast.14, f32[256,1024]{1,0:T(8,128)} %t_ref.1), custom_call_target="tpu_custom_call" | custom-call | tf_op jit(solution)/shard_map/step/pallas_call | solution.py:388
  40.9 2.6 %update.1 = (f32[256,1024]{1,0:T(8,128)}, f32[8,128]{1,0:T(8,128)}, f32[64,256]{1,0:T(8,128)}) custom-call(bf16[256,512]{1,0:T(8,128)(2,1)S(1)} %get-tuple-element.12.uh_ref, bf16[256,512]{1,0:T(8,128)(2,1)S(1)} %get-tuple-element.13.ul_ref, f32[2,8,2,64,256]{4,3,2,1,0:T(8,128)S(1)} %bitcast.13, f32[256,1024]{1,0:T(8,128)S(1)} %get-tuple-element.15.t_ref, ...), custom_call_target="tpu_custom_call" | custom-call | tf_op jit(solution)/shard_map/update/pallas_call | solution.py:439

commit v4 on v3

--- a/solution.py
+++ b/solution.py
@@ -57,7 +57,7 @@
     out = []
     while e > tol:
         m = 2.0 / (2.0 - e * e)
-        out.append(m)
+        out.append((m, e))
         e = e * e * m / 2.0
     return 2.0 / (1.0 + top), out
 
@@ -69,19 +69,75 @@
 
 
 TOL = {256: 3e-4, 128: 1e-3, 64: 1e-3, 32: 1e-3, 16: 1e-3}
-BASE = 16
+SMALL = 0.05
+BASE = 32
+GROUP = 4
 
 
 def half_split(m, n, dot, dot_t):
     i, j = grid2(n)
+    one = jnp.where(i == j, 1.0, 0.0)
     start, steps = scales(1.0 + n, TOL[n])
     zs = [start * x[:, :n] for x in m]
-    for k, s in enumerate(steps):
-        ns = [jnp.where(i == j, 2.0 * s, 0.0) - s * z[:n] for z in zs]
+    for k, (s, e) in enumerate(steps):
+        if e < SMALL:
+            ns = [(s * (one - z[:n])).astype(BF16) for z in zs]
+        else:
+            ns = [(2.0 * s) * one - s * z[:n] for z in zs]
         if k == len(steps) - 1:
             zs = [z[n:] for z in zs]
-        zs = [dot(z, nn) for z, nn in zip(zs, ns)]
+        if e < SMALL:
+            zs = [s * z + mm(z.astype(BF16), nn, NN) for z, nn in zip(zs, ns)]
+        else:
+            zs = [dot(z, nn) for z, nn in zip(zs, ns)]
     return zs, [x[n:, n:] - dot_t(z, x[n:, :n]) for x, z in zip(m, zs)]
+
+
+def high_low(z, first):
+    high = z.astype(BF16).astype(F32)
+    out = jnp.where(first, high, z - high).astype(BF16)
+    return jnp.concatenate([out, out], 1)
+
+
+def twice(n, b):
+    rows = []
+    for k in range(0, 128, 2 * b):
+        rows += [n[k:k + b]] * 2
+    return jnp.concatenate(rows, 0)
+
+
+def dot_pair(hl, n, b):
+    high = n.astype(BF16).astype(F32)
+    w = jnp.concatenate([twice(high, b).astype(BF16), twice(n - high, b).astype(BF16)], 0)
+    return mm(hl, w, NN)
+
+
+def tile_split(tiles, ts, b):
+    i, j = grid2(128)
+    bi, bj = i // b, j // b
+    pair = i // (2 * b) == j // (2 * b)
+    even = bi % 2 == 0
+    first = bj % 2 == 0
+    unit = jnp.where(jnp.logical_and(jnp.logical_and(pair, even), i % b == j % b), 1.0, 0.0)
+    start, steps = scales(1.0 + b, TOL[b])
+    doubled = [jnp.where(pair, jnp.where(first, m, pltpu.roll(m, b, 1)), 0.0) for m in tiles]
+    zs = [start * d for d in doubled]
+    for s, e in steps:
+        if e < SMALL:
+            ns = [jnp.where(even, s * (unit - z), 0.0).astype(BF16) for z in zs]
+            zs = [s * z + mm(z.astype(BF16), nn, NN) for z, nn in zip(zs, ns)]
+        else:
+            ns = [(2.0 * s) * unit - s * z for z in zs]
+            zs = [dot_pair(high_low(z, first), nn, b) for z, nn in zip(zs, ns)]
+    gs = [high_low(jnp.where(even, 0.0, z), first) for z in zs]
+    out = []
+    for m, g, d in zip(tiles, gs, doubled):
+        lows = split(jnp.where(even, 0.0, d))
+        out.append(jnp.where(bi == bj, m, 0.0) - mm(g, jnp.concatenate(lows, 1), NT))
+    if ts is None:
+        g_only = [jnp.where(jnp.logical_and(first, jnp.logical_not(even)), z, 0.0) for z in zs]
+        return out, [jnp.where(i == j, 1.0, 0.0) - g for g in g_only]
+    return out, [t - dot_pair(g, t, b) for t, g in zip(ts, gs)]
 
 
 def base_factors(tiles):
@@ -97,49 +153,38 @@
         rows.append(acc)
     ident = jnp.where(sub == lane % BASE, 1.0, 0.0)
     es = [ident] * len(tiles)
-    for p in range(BASE):
-        index = (lane // BASE) * BASE + p
+    for p0 in range(0, BASE, GROUP):
+        index = [(lane // BASE) * BASE + p0 + c for c in range(GROUP)]
         for t in range(len(tiles)):
-            col = jnp.take_along_axis(rows[t], index, axis=1, mode="promise_in_bounds")
-            root = lax.rsqrt(col[p:p + 1])
-            e_row = es[t][p:p + 1] * root
-            if p < BASE - 1:
-                a_row = rows[t][p:p + 1] * (root * root)
-                below = jnp.where(sub > p, col, 0.0)
-                rows[t] = rows[t] - below * a_row
+            cols = [jnp.take_along_axis(rows[t], i, axis=1, mode="promise_in_bounds")
+                    for i in index]
+            for c in range(GROUP):
+                p = p0 + c
+                root = lax.rsqrt(cols[c][p:p + 1])
+                e_row = es[t][p:p + 1] * root
+                if p == BASE - 1:
+                    es[t] = jnp.where(sub == p, e_row, es[t])
+                    break
+                inv = root * root
+                below = jnp.where(sub > p, cols[c], 0.0)
+                for q in range(c + 1, GROUP):
+                    cols[q] = cols[q] - below * (cols[q][p:p + 1] * inv)
+                if p0 + GROUP < BASE:
+                    rows[t] = rows[t] - below * (rows[t][p:p + 1] * inv)
                 es[t] = jnp.where(sub == p, e_row, es[t] - below * (e_row * root))
-            else:
-                es[t] = jnp.where(sub == p, e_row, es[t])
     return [jnp.concatenate([jnp.where(lane // BASE == g, e, 0.0) for g in range(groups)], 0)
             for e in es]
 
 
 def factor_inverse(a, between=lambda: None):
-    (g1,), (s,) = half_split([a[...]], 256, dot3, lambda x, y: dot3(x, y, NT))
-    blocks = [a[0:256, 0:256], s]
+    (g1,), (s,) = half_split([a()], 256, dot3, lambda x, y: dot3(x, y, NT))
+    blocks = [a()[:256, :256], s]
     g2, s2 = half_split(blocks, 128, dotp, dotp_t)
     tiles = [blocks[0][:128, :128], s2[0], blocks[1][:128, :128], s2[1]]
-    i, j = grid2(128)
     ts = None
     b = 64
     while b >= BASE:
-        bi, bj = i // b, j // b
-        start, steps = scales(1.0 + b, TOL[b])
-        pair = jnp.logical_and(i // (2 * b) == j // (2 * b), bj % 2 == 0)
-        even = bi % 2 == 0
-        low = jnp.logical_and(pair, jnp.logical_not(even))
-        diag = jnp.logical_and(i == j, even)
-        lows = [jnp.where(low, m, 0.0) for m in tiles]
-        zs = [jnp.where(pair, start * m, 0.0) for m in tiles]
-        for sc in steps:
-            ns = [jnp.where(diag, 2.0 * sc, 0.0) - jnp.where(even, sc * z, 0.0) for z in zs]
-            zs = [dotp(z, nn) for z, nn in zip(zs, ns)]
-        gs = [jnp.where(even, 0.0, z) for z in zs]
-        tiles = [jnp.where(bi == bj, m, 0.0) - dotp_t(g, lo) for m, g, lo in zip(tiles, gs, lows)]
-        if ts is None:
-            ts = [jnp.where(i == j, 1.0, 0.0) - g for g in gs]
-        else:
-            ts = [t - dotp(g, t) for t, g in zip(ts, gs)]
+        tiles, ts = tile_split(tiles, ts, b)
         b //= 2
     g1p = jnp.concatenate([g1[:128], g1[128:] - dotp(g2[1], g1[:128])], 0)
     bases = base_factors(tiles)
@@ -154,7 +199,7 @@
     i, j = grid2(256)
     one = jnp.where(i == j, 1.0, 0.0)
     low_half = jnp.where(i > j, 1.0, jnp.where(i == j, 0.5, 0.0))
-    a_s = split(a[...])
+    a_s = split(a())
     w1s = split(w11)
     w2s = split(jnp.concatenate([w21, w22], 1))
     wa1 = split(dot3s(w1s, [x[:256, :256] for x in a_s]))
@@ -168,7 +213,7 @@
 
 
 def step_kernel(d_ref, b_ref, t_ref, bc_ref, fd_ref, fp_ref, uh_ref, ul_ref, to_ref,
-                g_ref, br_ref, m_ref, a4_ref, a_ref, w_ref, l_ref, bt_ref,
+                g_ref, br_ref, m_ref, a4_ref, p_ref, bt_ref,
                 az_s, az_r, ax_s, ax_r, ay_s, ay_r, ac_s, ac_r,
                 bz_s, bz_r, mv_s, mv_r, bx_s, bx_r, by_s, by_r, bk_s, bk_r, loc_sem):
     row = lax.axis_index("row")
@@ -322,16 +367,20 @@
     b_yx = fan(bc_ref.at[core, :, x, bhi], bx_s, bx_r, 3, at_x, 3)
     for c in b_yx:
         c.start()
+    def place(k):
+        for c in range(CHIPS):
+            for s in range(2):
+                for l in range(4):
+                    a4_ref[l, pl.ds(32 * c + 16 * k + s, 8, stride=2), :] = (
+                        g_ref[c // 4, c % 4, k, :, 2 * l + s, :])
+
+    place(core)
     for c in a_c:
         c.wait()
-
-    for r in range(2 * CHIPS):
-        for s in range(2):
-            for l in range(4):
-                a4_ref[l, pl.ds(16 * r + s, 8, stride=2), :] = (
-                    g_ref[r // 8, r // 2 % 4, r % 2, :, 2 * l + s, :])
-    for l in range(4):
-        a_ref[:, l * 128:(l + 1) * 128] = a4_ref[l]
+    place(1 - core)
+
+    def block():
+        return jnp.concatenate([a4_ref[l] for l in range(4)], 1)
 
     b_c = []
 
@@ -348,34 +397,30 @@
             b_yx[k - 1].wait()
             b_c.append(to_partner(bc_ref.at[core, :, (x + 4 - k) % 4, bhi], bk_s, bk_r, 4 + k))
 
-    w11, w21, w22 = factor_inverse(a_ref, between)
-    w_ref[0:256, 0:256] = w11
-    w_ref[0:256, 256:512] = jnp.zeros((256, 256), F32)
-    w_ref[256:512, 0:256] = w21
-    w_ref[256:512, 256:512] = w22
-
+    w11, w21, w22 = factor_inverse(block, between)
     w1s = split(w11)
     w2s = split(jnp.concatenate([w21, w22], 1))
     d = row * COLS + z
-    mine = split(a_ref[pl.ds(pl.multiple_of((d // 4) * 8, 8), 8), :])
-    l_ref[:, 0:256] = dot3s([v[:, :256] for v in mine], w1s, NT)
-    l_ref[:, 256:512] = dot3s(mine, w2s, NT)
+    sixteen = pl.ds(pl.multiple_of((d // 8) * 16, 16), 16)
+    mine = split(jnp.concatenate([a4_ref[l, sixteen, :] for l in range(4)], 1))
+    b_s = [jnp.concatenate(v, 0) for v in zip(split(bt_ref[...]), mine)]
+    p1 = dot3s([v[:, :256] for v in b_s], w1s, NT)
+    p2 = dot3s(b_s, w2s, NT)
+    p_ref[:, 0:256] = p1
+    p_ref[:, 256:512] = p2
+    p2s = split(p2[:256])
+    u2 = dot3s(p2s, w2s)
+    u1 = u2[:, :256] + dot3s(split(p1[:256]), w1s)
+    for cols, u in ((slice(0, 256), u1), (slice(256, 512), u2[:, 256:])):
+        uh_ref[:, cols], ul_ref[:, cols] = split(u)
     lane = lax.broadcasted_iota(jnp.int32, (1, 512), 1)
     for s in range(2):
-        line_s = l_ref[pl.ds(2 * (d % 4) + s, 1), :]
+        line_s = p_ref[pl.ds(256 + 2 * (d % 8) + s, 1), :]
         line_s = jnp.where(lane <= 2 * d + s, line_s, 0.0)
         for l in range(4):
             fd_ref[2 * l + s:2 * l + s + 1, :] = line_s[:, l * 128:(l + 1) * 128]
-
-    fp_ref[...] = dot3(w_ref[pl.ds(pl.multiple_of(z * 64, 64), 64), :],
-                       br_ref[...].reshape(512, 256))
-    b_s = split(bt_ref[...])
-    p1 = split(dot3s([v[:, :256] for v in b_s], w1s, NT))
-    p2 = split(dot3s(b_s, w2s, NT))
-    u2 = dot3s(p2, w2s)
-    u1 = u2[:, :256] + dot3s(p1, w1s)
-    for cols, u in ((slice(0, 256), u1), (slice(256, 512), u2[:, 256:])):
-        uh_ref[:, cols], ul_ref[:, cols] = split(u)
+    part = p_ref[0:256, pl.ds(pl.multiple_of((z // 2) * 128, 128), 128)].T
+    fp_ref[...] = jnp.where(z % 2 == 0, part[:64], part[64:])
     own_t.wait()
     for c in b_c:
         c.wait()
@@ -402,9 +447,7 @@
             pltpu.VMEM((COLS, 64, 256), F32),
             pltpu.VMEM((64, 256), F32),
             pltpu.VMEM((4, 512, 128), F32),
-            pltpu.VMEM((512, 512), F32),
-            pltpu.VMEM((512, 512), F32),
-            pltpu.VMEM((8, 512), F32),
+            pltpu.VMEM((272, 512), F32),
             pltpu.VMEM((256, 512), F32),
             *dma(7), *dma(6), *dma(6), *dma(8),
             *dma(7), *dma(2), *dma(6), *dma(6), *dma(8),

time: 43.9 us -> 41.9 us (0.954)
  Pallas kernels: 42.9 us -> 40.5 us
    pallas_call x1, Pallas kernels: 40.3 us -> 38 us  [step(): pl.pallas_call(step_kernel, out_shape=(jax.ShapeDtypeStruct((2, 4, 4, 64,...]
where the time goes in v4:
time: 41.9 us; the launch traced here: 41.2 us
  Pallas kernels  40.5 us (97%)
  between operations  0.64 us (2%)
    pallas_call x1, Pallas kernels, step(): pl.pallas_call(step_kernel, out_shape=(jax.ShapeDtypeStruct((2, 4, 4, 64,...  38 us
    pallas_call x1, Pallas kernels, update(): pl.pallas_call(update_kernel, out_shape=(jax.ShapeDtypeStruct((256, 1024)...  2.56 us

profile of v4, /device:TPU:1, one launch (start us, length us, event | category | flops | bytes accessed | tf_op | source)
XLA Modules:
  0.0 41.2 jit_solution(15459153770891931633)
XLA Ops:
  0.6 38.0 %step.1 = (f32[2,4,4,64,256]{4,3,2,1,0:T(8,128)S(1)}, f32[8,128]{1,0:T(8,128)S(1)}, f32[64,256]{1,0:T(8,128)S(1)}, bf16[256,512]{1,0:T(8,128)(2,1)S(1)}, bf16[25...) custom-call(f32[8,128]{1,0:T(8,128)} %bitcast.15, f32[64,256]{1,0:T(8,128)} %bitcast.14, f32[256,1024]{1,0:T(8,128)} %t_ref.1), custom_call_target="tpu_custom_call" | custom-call | tf_op jit(solution)/shard_map/step/pallas_call | solution.py:433
  38.6 2.6 %update.1 = (f32[256,1024]{1,0:T(8,128)}, f32[8,128]{1,0:T(8,128)}, f32[64,256]{1,0:T(8,128)}) custom-call(bf16[256,512]{1,0:T(8,128)(2,1)S(1)} %get-tuple-element.12.uh_ref, bf16[256,512]{1,0:T(8,128)(2,1)S(1)} %get-tuple-element.13.ul_ref, f32[2,8,2,64,256]{4,3,2,1,0:T(8,128)S(1)} %bitcast.13, f32[256,1024]{1,0:T(8,128)S(1)} %get-tuple-element.15.t_ref, ...), custom_call_target="tpu_custom_call" | custom-call | tf_op jit(solution)/shard_map/update/pallas_call | solution.py:482

commit v5 on v4

--- a/solution.py
+++ b/solution.py
@@ -69,7 +69,7 @@
 
 
 TOL = {256: 3e-4, 128: 1e-3, 64: 1e-3, 32: 1e-3, 16: 1e-3}
-SMALL = 0.05
+SMALL = 0.15
 BASE = 32
 GROUP = 4
 
@@ -247,7 +247,7 @@
                 for k in range(1, n + 1)]
 
     barrier = pltpu.get_barrier_semaphore()
-    for k in range(1, COLS):
+    for k in (4, 3, 5, 2, 6, 1, 7):
         pl.semaphore_signal(barrier, inc=1, device_id=at_z(k), device_id_type=MESH)
     for k in range(1, CHIPS):
         pl.semaphore_signal(barrier, inc=1, device_id=at_chip(k), device_id_type=MESH)
@@ -262,8 +262,8 @@
 
     a_z = [copy(d_ref, own_tile, az_s.at[k - 1], az_r.at[k - 1], at_z(k))
            for k in range(1, COLS)]
-    for c in a_z:
-        c.start()
+    for k in (4, 3, 5, 2, 6, 1, 7):
+        a_z[k - 1].start()
 
     move1 = copy(b_ref, m_ref, mv_s.at[0], mv_r.at[0], at_chip(2 * z))
     move1_own = pltpu.make_async_copy(b_ref, m_ref, loc_sem.at[2])
@@ -284,9 +284,9 @@
     lo, hi = pl.ds(0, 4), pl.ds(4, 4)
     a_x = fan(g_ref.at[y, x, core, lo], ax_s, ax_r, 0, at_x, 3)
     a_y = fan(g_ref.at[y, x, core, hi], ay_s, ay_r, 0, at_y, 3)
-    for p, q in zip(a_x, a_y):
-        p.start()
-        q.start()
+    for k in (1, 0, 2):
+        a_x[k].start()
+        a_y[k].start()
 
     @pl.when(z != 0)
     def _():
@@ -313,18 +313,13 @@
     for c in a_x:
         c.wait()
     a_xy = fan(g_ref.at[y, :, core, lo], ay_s, ay_r, 3, at_y, 3)
-    for c in a_xy:
-        c.start()
+    for k in (1, 0, 2):
+        a_xy[k].start()
     for c in a_y:
         c.wait()
     a_yx = fan(g_ref.at[:, x, core, hi], ax_s, ax_r, 3, at_x, 3)
-    for c in a_yx:
-        c.start()
-
-    b_z = [copy(b_ref, br_ref.at[z], bz_s.at[k - 1], bz_r.at[k - 1], at_z(k))
-           for k in range(1, COLS)]
-    for c in b_z:
-        c.start()
+    for k in (1, 0, 2):
+        a_yx[k].start()
 
     def to_partner(ref, ssem, rsem, k):
         c = copy(ref, ref, ssem.at[k], rsem.at[k], partner)
@@ -348,6 +343,11 @@
     for p, q in zip(b_x, b_y):
         p.start()
         q.start()
+
+    b_z = [copy(b_ref, br_ref.at[z], bz_s.at[k - 1], bz_r.at[k - 1], at_z(k))
+           for k in range(1, COLS)]
+    for c in b_z:
+        c.start()
 
     for k in range(1, 4):
         a_xy[k - 1].wait_recv()

time: 41.9 us -> 41.5 us (level); the launches traced: 41.2 us -> 41.4 us
  no operation moved by 1% of the time
where the time goes in v5:
time: 41.5 us; the launch traced here: 41.4 us
  Pallas kernels  40.8 us (98%)
  between operations  0.64 us (2%)
    pallas_call x1, Pallas kernels, step(): pl.pallas_call(step_kernel, out_shape=(jax.ShapeDtypeStruct((2, 4, 4, 64,...  38.2 us
    pallas_call x1, Pallas kernels, update(): pl.pallas_call(update_kernel, out_shape=(jax.ShapeDtypeStruct((256, 1024)...  2.55 us

profile of v5, /device:TPU:1, one launch (start us, length us, event | category | flops | bytes accessed | tf_op | source)
XLA Modules:
  0.0 41.4 jit_solution(1984241487729959647)
XLA Ops:
  0.6 38.2 %step.1 = (f32[2,4,4,64,256]{4,3,2,1,0:T(8,128)S(1)}, f32[8,128]{1,0:T(8,128)S(1)}, f32[64,256]{1,0:T(8,128)S(1)}, bf16[256,512]{1,0:T(8,128)(2,1)S(1)}, bf16[25...) custom-call(f32[8,128]{1,0:T(8,128)} %bitcast.15, f32[64,256]{1,0:T(8,128)} %bitcast.14, f32[256,1024]{1,0:T(8,128)} %t_ref.1), custom_call_target="tpu_custom_call" | custom-call | tf_op jit(solution)/shard_map/step/pallas_call | solution.py:433
  38.9 2.6 %update.1 = (f32[256,1024]{1,0:T(8,128)}, f32[8,128]{1,0:T(8,128)}, f32[64,256]{1,0:T(8,128)}) custom-call(bf16[256,512]{1,0:T(8,128)(2,1)S(1)} %get-tuple-element.12.uh_ref, bf16[256,512]{1,0:T(8,128)(2,1)S(1)} %get-tuple-element.13.ul_ref, f32[2,8,2,64,256]{4,3,2,1,0:T(8,128)S(1)} %bitcast.13, f32[256,1024]{1,0:T(8,128)S(1)} %get-tuple-element.15.t_ref, ...), custom_call_target="tpu_custom_call" | custom-call | tf_op jit(solution)/shard_map/update/pallas_call | solution.py:482

commit v6 on v5

--- a/solution.py
+++ b/solution.py
@@ -249,16 +249,23 @@
     barrier = pltpu.get_barrier_semaphore()
     for k in (4, 3, 5, 2, 6, 1, 7):
         pl.semaphore_signal(barrier, inc=1, device_id=at_z(k), device_id_type=MESH)
-    for k in range(1, CHIPS):
-        pl.semaphore_signal(barrier, inc=1, device_id=at_chip(k), device_id_type=MESH)
+    for k in (2, 1, 3):
+        pl.semaphore_signal(barrier, inc=1, device_id=at_x(k), device_id_type=MESH)
+        pl.semaphore_signal(barrier, inc=1, device_id=at_y(k), device_id_type=MESH)
     pl.semaphore_signal(barrier, inc=1, device_id=partner, device_id_type=MESH)
+
+    @pl.when(z != 0)
+    def _():
+        for k in (2 * z, CHIPS - 2 * z):
+            pl.semaphore_signal(barrier, inc=1, device_id=at_chip(k), device_id_type=MESH)
+
     own_tile = g_ref.at[y, x, core, z]
     own_a = pltpu.make_async_copy(d_ref, own_tile, loc_sem.at[0])
     own_b = pltpu.make_async_copy(b_ref, br_ref.at[z], loc_sem.at[1])
     own_t = pltpu.make_async_copy(t_ref, to_ref, loc_sem.at[4])
     own_a.start()
     own_b.start()
-    pl.semaphore_wait(barrier, COLS + CHIPS - 1)
+    pl.semaphore_wait(barrier, COLS + 6 + 2 * ((z + COLS - 1) // COLS))
 
     a_z = [copy(d_ref, own_tile, az_s.at[k - 1], az_r.at[k - 1], at_z(k))
            for k in range(1, COLS)]

time: 41.5 us -> 40.7 us (0.981)
  Pallas kernels: 40.8 us -> 40 us
    pallas_call x1, Pallas kernels: 38.2 us -> 37.4 us  [step(): pl.pallas_call(step_kernel, out_shape=(jax.ShapeDtypeStruct((2, 4, 4, 64,...]
where the time goes in v6:
time: 40.7 us; the launch traced here: 40.6 us
  Pallas kernels  40 us (98%)
  between operations  0.64 us (2%)
    pallas_call x1, Pallas kernels, step(): pl.pallas_call(step_kernel, out_shape=(jax.ShapeDtypeStruct((2, 4, 4, 64,...  37.4 us
    pallas_call x1, Pallas kernels, update(): pl.pallas_call(update_kernel, out_shape=(jax.ShapeDtypeStruct((256, 1024)...  2.56 us

profile of v6, /device:TPU:1, one launch (start us, length us, event | category | flops | bytes accessed | tf_op | source)
XLA Modules:
  0.0 40.6 jit_solution(14145000055646804595)
XLA Ops:
  0.6 37.4 %step.1 = (f32[2,4,4,64,256]{4,3,2,1,0:T(8,128)S(1)}, f32[8,128]{1,0:T(8,128)S(1)}, f32[64,256]{1,0:T(8,128)S(1)}, bf16[256,512]{1,0:T(8,128)(2,1)S(1)}, bf16[25...) custom-call(f32[8,128]{1,0:T(8,128)} %bitcast.15, f32[64,256]{1,0:T(8,128)} %bitcast.14, f32[256,1024]{1,0:T(8,128)} %t_ref.1), custom_call_target="tpu_custom_call" | custom-call | tf_op jit(solution)/shard_map/step/pallas_call | solution.py:440
  38.1 2.6 %update.1 = (f32[256,1024]{1,0:T(8,128)}, f32[8,128]{1,0:T(8,128)}, f32[64,256]{1,0:T(8,128)}) custom-call(bf16[256,512]{1,0:T(8,128)(2,1)S(1)} %get-tuple-element.12.uh_ref, bf16[256,512]{1,0:T(8,128)(2,1)S(1)} %get-tuple-element.13.ul_ref, f32[2,8,2,64,256]{4,3,2,1,0:T(8,128)S(1)} %bitcast.13, f32[256,1024]{1,0:T(8,128)S(1)} %get-tuple-element.15.t_ref, ...), custom_call_target="tpu_custom_call" | custom-call | tf_op jit(solution)/shard_map/update/pallas_call | solution.py:489
